TPU v7x, 512 devices: a whole 4x8x8 slice. The times are simulated.
512 devices in a mesh: space: 64 (over y_lo, z, core), band: 8 (over y_hi, x).
Axes of the slice: x: 4, y: 8 (y_hi: 2, y_lo: 4; y = y_hi * 4 + y_lo), z: 8, core: 2. Of those that a mesh axis runs over, the one named last changes fastest.
Arguments:
- bands: bfloat16 [16, 4, 128, 128, 128], P('band', None, 'space'), may hold values from -6 to 6
- occ_level: int32 [16], P('band'), may hold values from 1 to 4
- block_owner: int32 [1], replicated, may hold values from 0 to 15
Outputs:
- exchange: float32 [2, 4, 128, 128, 128], P(None, None, 'space', 'band')
All inputs are finite; a program needn't handle non-finite values.
Results may differ from a plain program's by a relative error of at most 0.0013.
Values may be sent and summed in bfloat16 or wider, within the bound.
No kernel may reach another device: no remote copies, remote signals or barrier semaphores. Data moves between devices by JAX's collectives and lax.ppermute only.
A program may use at most 64 MiB of HBM per device.

v0:
```python
import jax
import jax.numpy as jnp
from jax import lax
from jax.experimental import pallas as pl
from jax.experimental.pallas import tpu as pltpu
from jax.sharding import PartitionSpec as P


SWEEPS = 4
jacobi_diagonal = 6.5

H = SWEEPS - 1
RES = 2
COMPS = 4
PLANES = 2
LANES = 128
GROUPS = 8
ROWS = 16
WIN = ROWS + 2 * H
BODY = PLANES * RES * COMPS * WIN
SEND = BODY + 8
F32 = jnp.float32
BF16 = jnp.bfloat16


def rows_of(d):
    return d, WIN - d


def plane_row(p, k, c):
    return ((p * RES + k) * COMPS + c) * WIN


N1 = RES * COMPS * ((WIN - 2) + (WIN - 4))
N2 = RES * COMPS * (WIN - 6)
NF = RES * 2 * RES * 2 * ROWS


def near_row(k, c):
    return (k * COMPS + c) * (WIN - 2)


def mid_row(k, c):
    return RES * COMPS * (WIN - 2) + (k * COMPS + c) * (WIN - 4)


def far_row(k, c):
    return (k * COMPS + c) * (WIN - 6)


def face_row(k, q, f):
    return ((k * 2 * RES + q) * 2 + f) * ROWS


OUTER, INNER, IN1, IN2, IN3 = range(5)
D1, D2, D3 = jacobi_diagonal, jacobi_diagonal ** 2, jacobi_diagonal ** 3


def pack_kernel(core_ref, bands_hbm, occ_hbm, out_ref, raw, occ_ref, ext, flat, sems, occ_sem):
    x = raw.shape[1]
    core = core_ref[0]
    levels = pltpu.make_async_copy(occ_hbm, occ_ref, occ_sem)
    levels.start()
    copies = [pltpu.make_async_copy(bands_hbm.at[pl.ds(PLANES * m, PLANES)], raw.at[pl.ds(PLANES * m, PLANES)], sems.at[m])
              for m in range(RES * COMPS)]
    for copy in copies:
        copy.start()
    for m, copy in enumerate(copies):
        copy.wait()
        for p in range(PLANES):
            plane = core if p == 0 else 1 - core
            n = p * RES * COMPS + m
            t = raw[m * PLANES + plane].astype(F32)
            ext[n, 8:8 + x] = t
            ext[n, 0:8] = t[x - 8:x]
            ext[n, 8 + x:16 + x] = t[0:8]
    levels.wait()
    for k in range(RES):
        flat[BODY + 4 * k:BODY + 4 * k + 4] = jnp.full((4, LANES), occ_ref[k].astype(F32), F32)
    for b in range(GROUPS):
        for n in range(PLANES * RES * COMPS):
            flat[n * WIN:(n + 1) * WIN] = ext[n, ROWS * b + 8 - H:ROWS * b + 8 - H + WIN]
        out_ref[b] = flat[...].astype(BF16)


def cut_kernel(own_ref, wide_ref, in1_ref, in3_ref, s1, s4):
    def one(src, carry):
        wide_ref[src] = own_ref[src].astype(F32)
        for k in range(RES):
            for c in range(COMPS):
                a = plane_row(0, k, c)
                o = plane_row(1, k, c)
                q = near_row(k, c)
                s1[q:q + WIN - 2] = wide_ref[src, o + 1:o + WIN - 1]
                q = mid_row(k, c)
                s1[q:q + WIN - 4] = wide_ref[src, a + 2:a + WIN - 2]
                q = far_row(k, c)
                s4[q:q + WIN - 6] = wide_ref[src, a + 3:a + WIN - 3]
        in1_ref[src] = s1[...].astype(BF16)
        in3_ref[src] = s4[...].astype(BF16)
        return carry

    lax.fori_loop(0, GROUPS, one, 0)


def starts_of(lo, hi):
    out = list(range(lo, hi - 7, 8))
    if out[-1] + 8 < hi:
        out.append(hi - 8)
    return out


def span(m):
    return rows_of(max(m - INNER, 0))


CORE_ROWS = starts_of(H, H + ROWS)


def field(f0, fi, fi3, src, k, c, m, r):
    if m in (OUTER, INNER):
        q = plane_row(m, k, c) + r
        return f0[src, q:q + 8]
    if m == IN1:
        q = near_row(k, c) + r - 1
        return fi[q:q + 8]
    if m == IN2:
        q = mid_row(k, c) + r - 2
        return fi[q:q + 8]
    q = far_row(k, c) + r - 3
    return fi3[q:q + 8]


def take_block(owner_ref, blk, planes, get):
    first = owner_ref[0]
    group = first // RES
    swap = (first % RES) == 1
    for i, m in enumerate(planes):
        for r in starts_of(*span(m)):
            for c in range(COMPS):
                b0 = get(group, 0, c, m, r)
                b1 = get(group, 1, c, m, r)
                blk[0, i, c, r:r + 8] = jnp.where(swap, b1, b0)
                blk[1, i, c, r:r + 8] = jnp.where(swap, b0, b1)


def densities(a, b):
    re = (a[0] * b[0] + a[1] * b[1]) + (a[2] * b[2] + a[3] * b[3])
    im = (a[0] * b[1] - a[1] * b[0]) + (a[2] * b[3] - a[3] * b[2])
    return re, im


def turned(t):
    return pltpu.roll(t, 1, 1) + pltpu.roll(t, LANES - 1, 1)


def face_kernel(owner_ref, f0, in1_ref, den, face_ref, fi, blk, lap, us):
    def get(src, k, c, m, r):
        return field(f0, fi, None, src, k, c, m, r)

    planes = (OUTER, INNER, IN1)
    fi[...] = in1_ref[owner_ref[0] // RES].astype(F32)
    take_block(owner_ref, blk, planes, get)

    def one_group(src, carry):
        fi[...] = in1_ref[src].astype(F32)
        for k in range(RES):
            i = src * RES + k
            for m in planes:
                for r in starts_of(*span(m)):
                    a = [get(src, k, c, m, r) for c in range(COMPS)]
                    for j in range(RES):
                        re, im = densities(a, [blk[j, m, c, r:r + 8] for c in range(COMPS)])
                        den[i, 2 * j, m, r:r + 8] = re
                        den[i, 2 * j + 1, m, r:r + 8] = im
            for q in range(2 * RES):
                for r in starts_of(2, WIN - 2):
                    e0 = den[i, q, OUTER, r:r + 8]
                    plane = (den[i, q, OUTER, r - 1:r + 7] + den[i, q, OUTER, r + 1:r + 9]) + turned(e0)
                    lap[k, q, r:r + 8] = plane
                    us[k, q, r:r + 8] = (2.0 * D1) * e0 + 3.0 * (den[i, q, INNER, r:r + 8] + plane)
                fa, fb = [], []
                for r in CORE_ROWS:
                    e0 = den[i, q, OUTER, r:r + 8]
                    e1 = den[i, q, INNER, r:r + 8]
                    plane = (us[k, q, r - 1:r + 7] + us[k, q, r + 1:r + 9]) + turned(us[k, q, r:r + 8])
                    fa.append(((D2 + 3.0) * e0 + D1 * e1) + (den[i, q, IN1, r:r + 8] + plane))
                    fb.append((D1 * e0 + e1) + 3.0 * lap[k, q, r:r + 8])
                for f, t in ((0, fa), (1, fb)):
                    o = face_row(k, q, f)
                    face_ref[src, o:o + ROWS] = jnp.concatenate(t, axis=0).astype(BF16)
        return carry

    lax.fori_loop(0, GROUPS, one_group, 0)


def scale_of(f0, src, k):
    level = f0[src, BODY + 4 * k:BODY + 4 * k + 1]
    return jnp.broadcast_to(level * (-0.25 * 0.25 / jacobi_diagonal ** 4), (8, LANES))


def add_products(out_ref, p, o, a, v):
    for j in range(RES):
        re, im = v[2 * j], v[2 * j + 1]
        for s in range(2):
            out_ref[j, 2 * s, p, o:o + 8] += a[2 * s] * re - a[2 * s + 1] * im
            out_ref[j, 2 * s + 1, p, o:o + 8] += a[2 * s] * im + a[2 * s + 1] * re


def local_kernel(owner_ref, f0, in1_ref, in3_ref, den, out_ref, fi, fi3, blk, d2s, t2s, t1s):
    def get(src, k, c, m, r):
        return field(f0, fi, fi3, src, k, c, m, r)

    def widen(src):
        fi[...] = in1_ref[src].astype(F32)
        fi3[...] = in3_ref[src].astype(F32)

    planes = (IN2, IN3)
    widen(owner_ref[0] // RES)
    take_block(owner_ref, blk, planes, get)
    out_ref[...] = jnp.zeros(out_ref.shape, F32)
    mids = starts_of(1, WIN - 1)

    def one_group(src, carry):
        widen(src)
        for k in range(RES):
            i = src * RES + k
            for z, m in enumerate(planes):
                for r in starts_of(*span(m)):
                    a = [get(src, k, c, m, r) for c in range(COMPS)]
                    for j in range(RES):
                        re, im = densities(a, [blk[j, z, c, r:r + 8] for c in range(COMPS)])
                        d2s[2 * j, z, r:r + 8] = re
                        d2s[2 * j + 1, z, r:r + 8] = im
            scale = scale_of(f0, src, k)

            def at(q, m, r):
                if m in planes:
                    return d2s[q, m - IN2, r:r + 8]
                return den[i, q, m, r:r + 8]

            def pair(q, z, d, r):
                t = at(q, z + d, r)
                return t + at(q, z - d, r) if z - d >= OUTER else t

            for z in (OUTER, INNER):
                t0 = {}
                for q in range(2 * RES):
                    kept = []
                    for r in mids:
                        e0 = at(q, z, r)
                        e1 = pair(q, z, 1, r)
                        e2 = pair(q, z, 2, r)
                        plane = (at(q, z, r - 1) + at(q, z, r + 1)) + turned(e0)
                        t2 = (D1 * e0 + 3.0 * e1) + plane
                        t2s[q, z, r:r + 8] = t2
                        kept.append((t2, ((D2 + 6.0) * e0 + (2.0 * D1) * e1) + 3.0 * e2))
                    for r, (t2, a1) in zip(mids, kept):
                        plane = (t2s[q, z, r - 1:r + 7] + t2s[q, z, r + 1:r + 9]) + turned(t2)
                        t1s[q, z, r:r + 8] = a1 + plane
                    for r in CORE_ROWS:
                        a0 = ((D3 + 2.0 * D1) * at(q, z, r) + (D2 + 3.0) * pair(q, z, 1, r)) + (
                            D1 * pair(q, z, 2, r) + at(q, z + 3, r))
                        plane = (t1s[q, z, r - 1:r + 7] + t1s[q, z, r + 1:r + 9]) + turned(t1s[q, z, r:r + 8])
                        t0[q, r] = scale * (a0 + plane)
                for r in CORE_ROWS:
                    a = [get(src, k, c, z, r) for c in range(COMPS)]
                    add_products(out_ref, z, r - H, a, [t0[q, r] for q in range(2 * RES)])
        return carry

    lax.fori_loop(0, GROUPS, one_group, 0)


def join_kernel(core_ref, f0, face_ref, part, out_ref, acc):
    acc[...] = part[...]

    def one_group(src, carry):
        for k in range(RES):
            scale = scale_of(f0, src, k)
            for z in (OUTER, INNER):
                got = []
                for q in range(2 * RES):
                    o = face_row(k, q, z)
                    got.append(face_ref[src, o:o + ROWS].astype(F32))
                for n, r in enumerate(CORE_ROWS):
                    a = [field(f0, None, None, src, k, c, z, r) * scale for c in range(COMPS)]
                    add_products(acc, z, r - H, a, [t[8 * n:8 * n + 8] for t in got])
        return carry

    lax.fori_loop(0, GROUPS, one_group, 0)
    core = core_ref[0]
    for j in range(RES):
        for c in range(COMPS):
            out_ref[j, c, core] = acc[j, c, OUTER]
            out_ref[j, c, 1 - core] = acc[j, c, INNER]


INTERPRET = False
KEEP = True
GRANT = 16 * 1024 * 1024


def on_device(bands, occ_level, block_owner):
    smem = pl.BlockSpec(memory_space=pltpu.SMEM)
    vmem = pl.BlockSpec(memory_space=pltpu.VMEM)
    hbm = pl.BlockSpec(memory_space=pltpu.HBM if KEEP else pl.ANY)

    def made(shape, dtype):
        return pltpu.VMEM(shape, dtype) if KEEP else jax.ShapeDtypeStruct(shape, dtype)

    def kept(value):
        return pltpu.with_memory_space_constraint(value, pltpu.VMEM) if KEEP else value

    def in_hbm(value):
        return pltpu.with_memory_space_constraint(value, pltpu.HBM) if KEEP else value

    def call(kernel, out_shape, in_specs, scratch):
        out_specs = [vmem] * len(out_shape) if isinstance(out_shape, list) else vmem
        return pl.pallas_call(
            kernel, out_shape=out_shape, in_specs=in_specs, out_specs=out_specs,
            scratch_shapes=scratch, interpret=INTERPRET,
            compiler_params=pltpu.CompilerParams(vmem_limit_bytes=GRANT))

    x = bands.shape[3]
    place = lax.axis_index("space").astype(jnp.int32)
    core = (place & 1).reshape(1)
    send = call(
        pack_kernel, made((GROUPS, SEND, LANES), BF16), [smem, hbm, hbm],
        [pltpu.VMEM((RES * COMPS * PLANES, x, LANES), BF16), pltpu.SMEM((RES,), jnp.int32),
         pltpu.VMEM((PLANES * RES * COMPS, x + 16, LANES), F32), pltpu.VMEM((SEND, LANES), F32),
         pltpu.SemaphoreType.DMA((RES * COMPS,)), pltpu.SemaphoreType.DMA],
    )(core, in_hbm(bands.reshape(RES * COMPS * PLANES, x, LANES)), in_hbm(occ_level))
    own = kept(lax.all_to_all(send, "band", 0, 0, tiled=True))

    wide, in1, in3 = call(
        cut_kernel,
        [made((GROUPS, SEND, LANES), F32), made((GROUPS, N1, LANES), BF16), made((GROUPS, N2, LANES), BF16)],
        [vmem], [pltpu.VMEM((N1, LANES), F32), pltpu.VMEM((N2, LANES), F32)],
    )(own)
    wide = kept(wide)
    count = lax.axis_size("space")

    def shift(value, even, odd):
        pairs = [(i, (i + (odd if i % 2 else even)) % count) for i in range(count)]
        value = lax.ppermute(value, "space", pairs)
        return kept(value)

    in1 = shift(in1, 1, -1)
    in3 = shift(in3, -2, 2)

    den, face = call(
        face_kernel,
        [made((GROUPS * RES, 2 * RES, 3, 24, LANES), F32), made((GROUPS, NF, LANES), BF16)],
        [smem] + [vmem] * 2,
        [pltpu.VMEM((N1, LANES), F32), pltpu.VMEM((RES, 3, COMPS, 24, LANES), F32),
         pltpu.VMEM((RES, 2 * RES, 24, LANES), F32), pltpu.VMEM((RES, 2 * RES, 24, LANES), F32)],
    )(block_owner, wide, in1)
    face = shift(face, -1, 1)

    part = call(
        local_kernel, made((RES, COMPS, PLANES, ROWS, LANES), F32),
        [smem] + [vmem] * 4,
        [pltpu.VMEM((N1, LANES), F32), pltpu.VMEM((N2, LANES), F32),
         pltpu.VMEM((RES, 2, COMPS, 24, LANES), F32)] + [pltpu.VMEM((2 * RES, 2, 24, LANES), F32)] * 3,
    )(block_owner, wide, in1, in3, kept(den))

    return call(
        join_kernel, jax.ShapeDtypeStruct((RES, COMPS, PLANES, ROWS, LANES), F32),
        [smem] + [vmem] * 3, [pltpu.VMEM((RES, COMPS, PLANES, ROWS, LANES), F32)],
    )(core, wide, face, kept(part))


def solution(mesh):
    return jax.shard_map(
        on_device,
        mesh=mesh,
        in_specs=(P("band", None, "space", None, None), P("band"), P()),
        out_specs=P(None, None, "space", "band", None),
        check_vma=False,
    )
```

profile of v0, /device:TPU:1, one launch (start us, length us, event | category | flops | bytes accessed | tf_op | source)
XLA Modules:
  0.0 67.1 jit_solution(9085180123525587183)
XLA Ops:
  0.0 1.3 %shard_map.37 = bf16[8,360,128]{2,1,0:T(8,128)(2,1)S(1)} custom-call(s32[1]{0:T(128)} %bitcast.core_ref, bf16[16,128,128]{2,1,0:T(8,128)(2,1)} %bitcast.2, s32[2]{0:T(128)} %occ_hbm.1), custom_call_target="tpu_custom_call" | custom-call | tf_op jit(solution)/shard_map/pallas_call | solution.py:327
  1.3 26.8 %all_to_all.5.own_ref = bf16[8,360,128]{2,1,0:T(8,128)(2,1)S(1)} all-to-all(bf16[8,360,128]{2,1,0:T(8,128)(2,1)S(1)} %shard_map.37), channel_id=1, replica_groups=mesh['space'=64,'band'=8] {'band'}, dimensions={0} | all-to-all | bytes 1474560 | tf_op jit(solution)/shard_map/all_to_all | solution.py:333
  28.1 0.3 shard_map.38
  28.4 6.5 %collective-permute-start = (bf16[8,304,128]{2,1,0:T(8,128)(2,1)S(1)}, bf16[8,304,128]{2,1,0:T(8,128)(2,1)S(1)}, u32[]{:S(2)}, u32[]{:S(2)}) collective-permute-start(bf16[8,304,128]{2,1,0:T(8,128)(2,1)S(1)} %get-tuple-element.11), channel_id=1, source_target_pairs={{0,8},{8,0},{16,24},{24,16},{32,40},{40,32},{48,56},{56,48},{64,72... | collective-permute-start | bytes 1867784 | tf_op jit(solution)/shard_map/ppermute | solution.py:345
  35.6 1.0 %collective-permute-done.in1_ref = bf16[8,304,128]{2,1,0:T(8,128)(2,1)S(1)} collective-permute-done((bf16[8,304,128]{2,1,0:T(8,128)(2,1)S(1)}, bf16[8,304,128]{2,1,0:T(8,128)(2,1)S(1)}, u32[]{:S(2)}, u32[]{:S(2)}) %collective-permute-start) | collective-permute-done | bytes 622624 | tf_op jit(solution)/shard_map/ppermute | solution.py:345
  36.6 2.0 %shard_map.39 = (f32[16,4,3,24,128]{4,3,2,1,0:T(8,128)S(1)}, bf16[8,256,128]{2,1,0:T(8,128)(2,1)S(1)}) custom-call(s32[1]{0:T(128)S(6)} %copy.4.owner_ref, f32[8,360,128]{2,1,0:T(8,128)S(1)} %get-tuple-element.10.f0, bf16[8,304,128]{2,1,0:T(8,128)(2,1)S(1)} %collective-permute-done.in1_ref), custom_call_target="tpu_custom_call" | custom-call | tf_op jit(solution)/shard_map/pallas_call | solution.py:351
  38.6 4.3 %collective-permute-start.1 = (bf16[8,256,128]{2,1,0:T(8,128)(2,1)S(1)}, bf16[8,256,128]{2,1,0:T(8,128)(2,1)S(1)}, u32[]{:S(2)}, u32[]{:S(2)}) collective-permute-start(bf16[8,256,128]{2,1,0:T(8,128)(2,1)S(1)} %get-tuple-element.12), channel_id=1, source_target_pairs={{0,504},{8,16},{16,8},{24,32},{32,24},{40,48},{48,40},{56,64},{64,... | collective-permute-start | bytes 1572872 | tf_op jit(solution)/shard_map/ppermute | solution.py:345
  42.9 4.0 %collective-permute-start.2 = (bf16[8,128,128]{2,1,0:T(8,128)(2,1)S(1)}, bf16[8,128,128]{2,1,0:T(8,128)(2,1)S(1)}, u32[]{:S(2)}, u32[]{:S(2)}) collective-permute-start(bf16[8,128,128]{2,1,0:T(8,128)(2,1)S(1)} %get-tuple-element.13), channel_id=1, source_target_pairs={{0,496},{8,24},{16,0},{24,40},{32,16},{40,56},{48,32},{56,72},{64,... | collective-permute-start | bytes 786440 | tf_op jit(solution)/shard_map/ppermute | solution.py:345
  46.9 13.4 %collective-permute-done.2.in3_ref = bf16[8,128,128]{2,1,0:T(8,128)(2,1)S(1)} collective-permute-done((bf16[8,128,128]{2,1,0:T(8,128)(2,1)S(1)}, bf16[8,128,128]{2,1,0:T(8,128)(2,1)S(1)}, u32[]{:S(2)}, u32[]{:S(2)}) %collective-permute-start.2) | collective-permute-done | bytes 262176 | tf_op jit(solution)/shard_map/ppermute | solution.py:345
  60.3 5.7 %shard_map.40.part = f32[2,4,2,16,128]{4,3,2,1,0:T(8,128)S(1)} custom-call(s32[1]{0:T(128)S(6)} %copy.4.owner_ref, f32[8,360,128]{2,1,0:T(8,128)S(1)} %get-tuple-element.10.f0, bf16[8,304,128]{2,1,0:T(8,128)(2,1)S(1)} %collective-permute-done.in1_ref, bf16[8,128,128]{2,1,0:T(8,128)(2,1)S(1)} %collective-permute-done.2.in3_ref, ...), custom_call_target="tpu_custom_call" | custom-call | tf_op jit(solution)/shard_map/pallas_call | solution.py:360
  66.0 0.0 collective-permute-done.1.face_ref
  66.0 1.1 %shard_map.41 = f32[2,4,2,16,128]{4,3,2,1,0:T(8,128)} custom-call(s32[1]{0:T(128)} %bitcast.core_ref, f32[8,360,128]{2,1,0:T(8,128)S(1)} %get-tuple-element.10.f0, bf16[8,256,128]{2,1,0:T(8,128)(2,1)S(1)} %collective-permute-done.1.face_ref, f32[2,4,2,16,128]{4,3,2,1,0:T(8,128)S(1)} %shard_map.40.part), custom_call_target="tpu_custom_call" | custom-call | tf_op jit(solution)/shard_map/pallas_call | solution.py:367
Async XLA Ops:
  28.4 8.2 %collective-permute-start = (bf16[8,304,128]{2,1,0:T(8,128)(2,1)S(1)}, bf16[8,304,128]{2,1,0:T(8,128)(2,1)S(1)}, u32[]{:S(2)}, u32[]{:S(2)}) collective-permute-start(bf16[8,304,128]{2,1,0:T(8,128)(2,1)S(1)} %get-tuple-element.11), channel_id=1, source_target_pairs={{0,8},{8,0},{16,24},{24,16},{32,40},{40,32},{48,56},{56,48},{64,72... | collective-permute-start | bytes 1867784 | tf_op jit(solution)/shard_map/ppermute | solution.py:345
  38.6 27.4 %collective-permute-start.1 = (bf16[8,256,128]{2,1,0:T(8,128)(2,1)S(1)}, bf16[8,256,128]{2,1,0:T(8,128)(2,1)S(1)}, u32[]{:S(2)}, u32[]{:S(2)}) collective-permute-start(bf16[8,256,128]{2,1,0:T(8,128)(2,1)S(1)} %get-tuple-element.12), channel_id=1, source_target_pairs={{0,504},{8,16},{16,8},{24,32},{32,24},{40,48},{48,40},{56,64},{64,... | collective-permute-start | bytes 1572872 | tf_op jit(solution)/shard_map/ppermute | solution.py:345
  42.9 17.5 %collective-permute-start.2 = (bf16[8,128,128]{2,1,0:T(8,128)(2,1)S(1)}, bf16[8,128,128]{2,1,0:T(8,128)(2,1)S(1)}, u32[]{:S(2)}, u32[]{:S(2)}) collective-permute-start(bf16[8,128,128]{2,1,0:T(8,128)(2,1)S(1)} %get-tuple-element.13), channel_id=1, source_target_pairs={{0,496},{8,24},{16,0},{24,40},{32,16},{40,56},{48,32},{56,72},{64,... | collective-permute-start | bytes 786440 | tf_op jit(solution)/shard_map/ppermute | solution.py:345
where the time goes:
time: 67.4 us; the launch traced here: 67.1 us
  blocking collectives  26.8 us (40%)
  starting transfers between devices  14.8 us (22%)
  waiting for transfers between devices  14.5 us (22%)
  Pallas kernels  10.4 us (15%)
  between operations  0.71 us (1%)
    all_to_all x1, blocking collectives, on_device(): own = kept(lax.all_to_all(send, 'band', 0, 0, tiled=True))  26.8 us
    ppermute x3, starting transfers between devices, shift(): value = lax.ppermute(value, 'space', pairs)  14.8 us
    ppermute x3, waiting for transfers between devices, shift(): value = lax.ppermute(value, 'space', pairs)  14.5 us
    pallas_call x1, Pallas kernels, on_device(): call(local_kernel, made((RES, COMPS, PLANES, ROWS, LANES), F32), [smem] +...  5.66 us
    pallas_call x1, Pallas kernels, on_device(): call(face_kernel, [made((GROUPS * RES, 2 * RES, 3, 24, LANES), F32), made...  2.05 us
  transfers between devices with their start and end apart: 3, of which 2 were waited for; matrix products, arithmetic and copies ran while one was open for 0% of the time, Pallas kernels for 8%

commit v1 on v0

--- a/solution.py
+++ b/solution.py
@@ -154,16 +154,14 @@
     return pltpu.roll(t, 1, 1) + pltpu.roll(t, LANES - 1, 1)
 
 
-def face_kernel(owner_ref, f0, in1_ref, den, face_ref, fi, blk, lap, us):
+def own_face_kernel(owner_ref, f0, den, fab, blk, lap, us):
     def get(src, k, c, m, r):
-        return field(f0, fi, None, src, k, c, m, r)
-
-    planes = (OUTER, INNER, IN1)
-    fi[...] = in1_ref[owner_ref[0] // RES].astype(F32)
+        return field(f0, None, None, src, k, c, m, r)
+
+    planes = (OUTER, INNER)
     take_block(owner_ref, blk, planes, get)
 
     def one_group(src, carry):
-        fi[...] = in1_ref[src].astype(F32)
         for k in range(RES):
             i = src * RES + k
             for m in planes:
@@ -179,16 +177,42 @@
                     plane = (den[i, q, OUTER, r - 1:r + 7] + den[i, q, OUTER, r + 1:r + 9]) + turned(e0)
                     lap[k, q, r:r + 8] = plane
                     us[k, q, r:r + 8] = (2.0 * D1) * e0 + 3.0 * (den[i, q, INNER, r:r + 8] + plane)
-                fa, fb = [], []
-                for r in CORE_ROWS:
+                for n, r in enumerate(CORE_ROWS):
                     e0 = den[i, q, OUTER, r:r + 8]
                     e1 = den[i, q, INNER, r:r + 8]
                     plane = (us[k, q, r - 1:r + 7] + us[k, q, r + 1:r + 9]) + turned(us[k, q, r:r + 8])
-                    fa.append(((D2 + 3.0) * e0 + D1 * e1) + (den[i, q, IN1, r:r + 8] + plane))
-                    fb.append((D1 * e0 + e1) + 3.0 * lap[k, q, r:r + 8])
-                for f, t in ((0, fa), (1, fb)):
-                    o = face_row(k, q, f)
-                    face_ref[src, o:o + ROWS] = jnp.concatenate(t, axis=0).astype(BF16)
+                    o = face_row(k, q, 0) + 8 * n
+                    fab[src, o:o + 8] = ((D2 + 3.0) * e0 + D1 * e1) + plane
+                    o = face_row(k, q, 1) + 8 * n
+                    fab[src, o:o + 8] = (D1 * e0 + e1) + 3.0 * lap[k, q, r:r + 8]
+        return carry
+
+    lax.fori_loop(0, GROUPS, one_group, 0)
+
+
+def face_kernel(owner_ref, fab, in1_ref, den1, face_ref, fi, blk):
+    def get(src, k, c, m, r):
+        return field(None, fi, None, src, k, c, m, r)
+
+    fi[...] = in1_ref[owner_ref[0] // RES].astype(F32)
+    take_block(owner_ref, blk, (IN1,), get)
+
+    def one_group(src, carry):
+        near = RES * COMPS * (WIN - 2)
+        fi[0:near] = in1_ref[src, 0:near].astype(F32)
+        for k in range(RES):
+            i = src * RES + k
+            for r in starts_of(*span(IN1)):
+                a = [get(src, k, c, IN1, r) for c in range(COMPS)]
+                for j in range(RES):
+                    re, im = densities(a, [blk[j, 0, c, r:r + 8] for c in range(COMPS)])
+                    den1[i, 2 * j, r:r + 8] = re
+                    den1[i, 2 * j + 1, r:r + 8] = im
+            for q in range(2 * RES):
+                o = face_row(k, q, 0)
+                face_ref[src, o:o + ROWS] = (fab[src, o:o + ROWS] + den1[i, q, H:H + ROWS]).astype(BF16)
+                o = face_row(k, q, 1)
+                face_ref[src, o:o + ROWS] = fab[src, o:o + ROWS].astype(BF16)
         return carry
 
     lax.fori_loop(0, GROUPS, one_group, 0)
@@ -207,15 +231,14 @@
             out_ref[j, 2 * s + 1, p, o:o + 8] += a[2 * s] * im + a[2 * s + 1] * re
 
 
-def local_kernel(owner_ref, f0, in1_ref, in3_ref, den, out_ref, fi, fi3, blk, d2s, t2s, t1s):
+def local_kernel(owner_ref, f0, in1_ref, den, den1, out_ref, fi, blk, d2s, t2s, t1s):
     def get(src, k, c, m, r):
-        return field(f0, fi, fi3, src, k, c, m, r)
+        return field(f0, fi, None, src, k, c, m, r)
 
     def widen(src):
         fi[...] = in1_ref[src].astype(F32)
-        fi3[...] = in3_ref[src].astype(F32)
-
-    planes = (IN2, IN3)
+
+    planes = (IN2,)
     widen(owner_ref[0] // RES)
     take_block(owner_ref, blk, planes, get)
     out_ref[...] = jnp.zeros(out_ref.shape, F32)
@@ -235,8 +258,10 @@
             scale = scale_of(f0, src, k)
 
             def at(q, m, r):
-                if m in planes:
-                    return d2s[q, m - IN2, r:r + 8]
+                if m == IN2:
+                    return d2s[q, 0, r:r + 8]
+                if m == IN1:
+                    return den1[i, q, r:r + 8]
                 return den[i, q, m, r:r + 8]
 
             def pair(q, z, d, r):
@@ -259,8 +284,9 @@
                         plane = (t2s[q, z, r - 1:r + 7] + t2s[q, z, r + 1:r + 9]) + turned(t2)
                         t1s[q, z, r:r + 8] = a1 + plane
                     for r in CORE_ROWS:
-                        a0 = ((D3 + 2.0 * D1) * at(q, z, r) + (D2 + 3.0) * pair(q, z, 1, r)) + (
-                            D1 * pair(q, z, 2, r) + at(q, z + 3, r))
+                        a0 = ((D3 + 2.0 * D1) * at(q, z, r) + (D2 + 3.0) * pair(q, z, 1, r)) + D1 * pair(q, z, 2, r)
+                        if z + 3 <= IN2:
+                            a0 = a0 + at(q, z + 3, r)
                         plane = (t1s[q, z, r - 1:r + 7] + t1s[q, z, r + 1:r + 9]) + turned(t1s[q, z, r:r + 8])
                         t0[q, r] = scale * (a0 + plane)
                 for r in CORE_ROWS:
@@ -271,10 +297,16 @@
     lax.fori_loop(0, GROUPS, one_group, 0)
 
 
-def join_kernel(core_ref, f0, face_ref, part, out_ref, acc):
+def join_kernel(core_ref, owner_ref, f0, in3_ref, face_ref, part, out_ref, acc, fi3, blk):
+    def get(src, k, c, m, r):
+        return field(f0, None, fi3, src, k, c, m, r)
+
+    fi3[...] = in3_ref[owner_ref[0] // RES].astype(F32)
+    take_block(owner_ref, blk, (IN3,), get)
     acc[...] = part[...]
 
     def one_group(src, carry):
+        fi3[...] = in3_ref[src].astype(F32)
         for k in range(RES):
             scale = scale_of(f0, src, k)
             for z in (OUTER, INNER):
@@ -283,8 +315,15 @@
                     o = face_row(k, q, z)
                     got.append(face_ref[src, o:o + ROWS].astype(F32))
                 for n, r in enumerate(CORE_ROWS):
-                    a = [field(f0, None, None, src, k, c, z, r) * scale for c in range(COMPS)]
-                    add_products(acc, z, r - H, a, [t[8 * n:8 * n + 8] for t in got])
+                    v = [t[8 * n:8 * n + 8] for t in got]
+                    if z == INNER:
+                        far = [get(src, k, c, IN3, r) for c in range(COMPS)]
+                        for j in range(RES):
+                            re, im = densities(far, [blk[j, 0, c, r:r + 8] for c in range(COMPS)])
+                            v[2 * j] = v[2 * j] + re
+                            v[2 * j + 1] = v[2 * j + 1] + im
+                    a = [get(src, k, c, z, r) * scale for c in range(COMPS)]
+                    add_products(acc, z, r - H, a, v)
         return carry
 
     lax.fori_loop(0, GROUPS, one_group, 0)
@@ -346,28 +385,36 @@
         return kept(value)
 
     in1 = shift(in1, 1, -1)
-    in3 = shift(in3, -2, 2)
-
-    den, face = call(
+
+    den, fab = call(
+        own_face_kernel,
+        [made((GROUPS * RES, 2 * RES, 2, 24, LANES), F32), made((GROUPS, NF, LANES), F32)],
+        [smem, vmem],
+        [pltpu.VMEM((RES, 2, COMPS, 24, LANES), F32), pltpu.VMEM((RES, 2 * RES, 24, LANES), F32),
+         pltpu.VMEM((RES, 2 * RES, 24, LANES), F32)],
+    )(block_owner, wide)
+    den1, face = call(
         face_kernel,
-        [made((GROUPS * RES, 2 * RES, 3, 24, LANES), F32), made((GROUPS, NF, LANES), BF16)],
+        [made((GROUPS * RES, 2 * RES, 24, LANES), F32), made((GROUPS, NF, LANES), BF16)],
         [smem] + [vmem] * 2,
-        [pltpu.VMEM((N1, LANES), F32), pltpu.VMEM((RES, 3, COMPS, 24, LANES), F32),
-         pltpu.VMEM((RES, 2 * RES, 24, LANES), F32), pltpu.VMEM((RES, 2 * RES, 24, LANES), F32)],
-    )(block_owner, wide, in1)
+        [pltpu.VMEM((N1, LANES), F32), pltpu.VMEM((RES, 1, COMPS, 24, LANES), F32)],
+    )(block_owner, kept(fab), in1)
     face = shift(face, -1, 1)
 
     part = call(
         local_kernel, made((RES, COMPS, PLANES, ROWS, LANES), F32),
         [smem] + [vmem] * 4,
-        [pltpu.VMEM((N1, LANES), F32), pltpu.VMEM((N2, LANES), F32),
-         pltpu.VMEM((RES, 2, COMPS, 24, LANES), F32)] + [pltpu.VMEM((2 * RES, 2, 24, LANES), F32)] * 3,
-    )(block_owner, wide, in1, in3, kept(den))
+        [pltpu.VMEM((N1, LANES), F32), pltpu.VMEM((RES, 1, COMPS, 24, LANES), F32),
+         pltpu.VMEM((2 * RES, 1, 24, LANES), F32)] + [pltpu.VMEM((2 * RES, 2, 24, LANES), F32)] * 2,
+    )(block_owner, wide, in1, kept(den), kept(den1))
+    in3 = shift(in3, -2, 2)
 
     return call(
         join_kernel, jax.ShapeDtypeStruct((RES, COMPS, PLANES, ROWS, LANES), F32),
-        [smem] + [vmem] * 3, [pltpu.VMEM((RES, COMPS, PLANES, ROWS, LANES), F32)],
-    )(core, wide, face, kept(part))
+        [smem, smem] + [vmem] * 4,
+        [pltpu.VMEM((RES, COMPS, PLANES, ROWS, LANES), F32), pltpu.VMEM((N2, LANES), F32),
+         pltpu.VMEM((RES, 1, COMPS, 24, LANES), F32)],
+    )(core, block_owner, wide, in3, face, kept(part))
 
 
 def solution(mesh):

time: 67.4 us -> 61.2 us (0.908)
  waiting for transfers between devices: 14.5 us -> 8.18 us
    ppermute x3, waiting for transfers between devices: 14.5 us -> 8.18 us  [shift(): value = lax.ppermute(value, 'space', pairs)]
    pallas_call x1 -> x2, Pallas kernels: 2.05 us -> 2.42 us  [the longest x1 2 us: on_device(): call(own_face_kernel, [made((GROUPS * RES, 2 * RES, 2, 24, LANES), F32),...]
  transfers between devices with their start and end apart: 3 -> 3, of which waited for: 2 -> 1; matrix products, arithmetic and copies ran while one was open for 0% -> 0% of each run, Pallas kernels for 8% -> 13%
where the time goes in v1:
time: 61.2 us; the launch traced here: 61 us
  blocking collectives  26.8 us (44%)
  starting transfers between devices  14.4 us (24%)
  Pallas kernels  10.9 us (18%)
  waiting for transfers between devices  8.18 us (13%)
  between operations  0.71 us (1%)
    all_to_all x1, blocking collectives, on_device(): own = kept(lax.all_to_all(send, 'band', 0, 0, tiled=True))  26.8 us
    ppermute x3, starting transfers between devices, shift(): value = lax.ppermute(value, 'space', pairs)  14.4 us
    ppermute x3, waiting for transfers between devices, shift(): value = lax.ppermute(value, 'space', pairs)  8.18 us
    pallas_call x1, Pallas kernels, on_device(): call(local_kernel, made((RES, COMPS, PLANES, ROWS, LANES), F32), [smem] +...  5.63 us
    pallas_call x1, Pallas kernels, on_device(): call(own_face_kernel, [made((GROUPS * RES, 2 * RES, 2, 24, LANES), F32),...  2 us
    pallas_call x1, Pallas kernels, on_device(): call(pack_kernel, made((GROUPS, SEND, LANES), BF16), [smem, hbm, hbm], [p...  1.31 us
    pallas_call x1, Pallas kernels, on_device(): call(join_kernel, jax.ShapeDtypeStruct((RES, COMPS, PLANES, ROWS, LANES),...  1.25 us
  transfers between devices with their start and end apart: 3, of which 1 were waited for; matrix products, arithmetic and copies ran while one was open for 0% of the time, Pallas kernels for 13%

profile of v1, /device:TPU:1, one launch (start us, length us, event | category | flops | bytes accessed | tf_op | source)
XLA Modules:
  0.0 61.0 jit_solution(7084352945765971393)
XLA Ops:
  0.0 1.3 %shard_map.37 = bf16[8,360,128]{2,1,0:T(8,128)(2,1)S(1)} custom-call(s32[1]{0:T(128)} %bitcast.core_ref, bf16[16,128,128]{2,1,0:T(8,128)(2,1)} %bitcast.2, s32[2]{0:T(128)} %occ_hbm.1), custom_call_target="tpu_custom_call" | custom-call | tf_op jit(solution)/shard_map/pallas_call | solution.py:366
  1.3 26.8 %all_to_all.5.own_ref = bf16[8,360,128]{2,1,0:T(8,128)(2,1)S(1)} all-to-all(bf16[8,360,128]{2,1,0:T(8,128)(2,1)S(1)} %shard_map.37), channel_id=1, replica_groups=mesh['space'=64,'band'=8] {'band'}, dimensions={0} | all-to-all | bytes 1474560 | tf_op jit(solution)/shard_map/all_to_all | solution.py:372
  28.1 0.3 shard_map.38
  28.4 6.5 %collective-permute-start.1 = (bf16[8,304,128]{2,1,0:T(8,128)(2,1)S(1)}, bf16[8,304,128]{2,1,0:T(8,128)(2,1)S(1)}, u32[]{:S(2)}, u32[]{:S(2)}) collective-permute-start(bf16[8,304,128]{2,1,0:T(8,128)(2,1)S(1)} %get-tuple-element.15), channel_id=1, source_target_pairs={{0,8},{8,0},{16,24},{24,16},{32,40},{40,32},{48,56},{56,48},{64,72... | collective-permute-start | bytes 1867784 | tf_op jit(solution)/shard_map/ppermute | solution.py:384
  35.6 2.0 %shard_map.39 = (f32[16,4,2,24,128]{4,3,2,1,0:T(8,128)S(1)}, f32[8,256,128]{2,1,0:T(8,128)S(1)}) custom-call(s32[1]{0:T(128)S(6)} %copy.4.owner_ref, f32[8,360,128]{2,1,0:T(8,128)S(1)} %get-tuple-element.12.f0), custom_call_target="tpu_custom_call" | custom-call | tf_op jit(solution)/shard_map/pallas_call | solution.py:389
  37.6 0.0 collective-permute-done.1.in1_ref
  37.6 0.4 shard_map.40
  38.0 3.9 %collective-permute-start.2 = (bf16[8,256,128]{2,1,0:T(8,128)(2,1)S(1)}, bf16[8,256,128]{2,1,0:T(8,128)(2,1)S(1)}, u32[]{:S(2)}, u32[]{:S(2)}) collective-permute-start(bf16[8,256,128]{2,1,0:T(8,128)(2,1)S(1)} %get-tuple-element.16), channel_id=1, source_target_pairs={{0,504},{8,16},{16,8},{24,32},{32,24},{40,48},{48,40},{56,64},{64,... | collective-permute-start | bytes 1572872 | tf_op jit(solution)/shard_map/ppermute | solution.py:384
  41.9 4.0 %collective-permute-start = (bf16[8,128,128]{2,1,0:T(8,128)(2,1)S(1)}, bf16[8,128,128]{2,1,0:T(8,128)(2,1)S(1)}, u32[]{:S(2)}, u32[]{:S(2)}) collective-permute-start(bf16[8,128,128]{2,1,0:T(8,128)(2,1)S(1)} %get-tuple-element.13), channel_id=1, source_target_pairs={{0,496},{8,24},{16,0},{24,40},{32,16},{40,56},{48,32},{56,72},{64,... | collective-permute-start | bytes 786440 | tf_op jit(solution)/shard_map/ppermute | solution.py:384
  45.9 5.6 %shard_map.41.part = f32[2,4,2,16,128]{4,3,2,1,0:T(8,128)S(1)} custom-call(s32[1]{0:T(128)S(6)} %copy.4.owner_ref, f32[8,360,128]{2,1,0:T(8,128)S(1)} %get-tuple-element.12.f0, bf16[8,304,128]{2,1,0:T(8,128)(2,1)S(1)} %collective-permute-done.1.in1_ref, f32[16,4,2,24,128]{4,3,2,1,0:T(8,128)S(1)} %get-tuple-element.17.den, ...), custom_call_target="tpu_custom_call" | custom-call | tf_op jit(solution)/shard_map/pallas_call | solution.py:404
  51.5 8.2 %collective-permute-done.in3_ref = bf16[8,128,128]{2,1,0:T(8,128)(2,1)S(1)} collective-permute-done((bf16[8,128,128]{2,1,0:T(8,128)(2,1)S(1)}, bf16[8,128,128]{2,1,0:T(8,128)(2,1)S(1)}, u32[]{:S(2)}, u32[]{:S(2)}) %collective-permute-start) | collective-permute-done | bytes 262176 | tf_op jit(solution)/shard_map/ppermute | solution.py:384
  59.7 0.0 collective-permute-done.2.face_ref
  59.7 1.3 %shard_map.42 = f32[2,4,2,16,128]{4,3,2,1,0:T(8,128)} custom-call(s32[1]{0:T(128)} %bitcast.core_ref, s32[1]{0:T(128)S(6)} %copy.4.owner_ref, f32[8,360,128]{2,1,0:T(8,128)S(1)} %get-tuple-element.12.f0, bf16[8,128,128]{2,1,0:T(8,128)(2,1)S(1)} %collective-permute-done.in3_ref, bf16[8,256,128]{2,1,0:T(8,128)(2,1)S(1)} %collective-permute-done.2.face_ref, ...), custom_call_target="tpu_custom_call" | custom-call | tf_op jit(solution)/shard_map/pallas_call | solution.py:412
Async XLA Ops:
  28.4 9.2 %collective-permute-start.1 = (bf16[8,304,128]{2,1,0:T(8,128)(2,1)S(1)}, bf16[8,304,128]{2,1,0:T(8,128)(2,1)S(1)}, u32[]{:S(2)}, u32[]{:S(2)}) collective-permute-start(bf16[8,304,128]{2,1,0:T(8,128)(2,1)S(1)} %get-tuple-element.15), channel_id=1, source_target_pairs={{0,8},{8,0},{16,24},{24,16},{32,40},{40,32},{48,56},{56,48},{64,72... | collective-permute-start | bytes 1867784 | tf_op jit(solution)/shard_map/ppermute | solution.py:384
  38.0 21.7 %collective-permute-start.2 = (bf16[8,256,128]{2,1,0:T(8,128)(2,1)S(1)}, bf16[8,256,128]{2,1,0:T(8,128)(2,1)S(1)}, u32[]{:S(2)}, u32[]{:S(2)}) collective-permute-start(bf16[8,256,128]{2,1,0:T(8,128)(2,1)S(1)} %get-tuple-element.16), channel_id=1, source_target_pairs={{0,504},{8,16},{16,8},{24,32},{32,24},{40,48},{48,40},{56,64},{64,... | collective-permute-start | bytes 1572872 | tf_op jit(solution)/shard_map/ppermute | solution.py:384
  41.9 17.8 %collective-permute-start = (bf16[8,128,128]{2,1,0:T(8,128)(2,1)S(1)}, bf16[8,128,128]{2,1,0:T(8,128)(2,1)S(1)}, u32[]{:S(2)}, u32[]{:S(2)}) collective-permute-start(bf16[8,128,128]{2,1,0:T(8,128)(2,1)S(1)} %get-tuple-element.13), channel_id=1, source_target_pairs={{0,496},{8,24},{16,0},{24,40},{32,16},{40,56},{48,32},{56,72},{64,... | collective-permute-start | bytes 786440 | tf_op jit(solution)/shard_map/ppermute | solution.py:384

commit v2 on v1

--- a/solution.py
+++ b/solution.py
@@ -297,16 +297,10 @@
     lax.fori_loop(0, GROUPS, one_group, 0)
 
 
-def join_kernel(core_ref, owner_ref, f0, in3_ref, face_ref, part, out_ref, acc, fi3, blk):
-    def get(src, k, c, m, r):
-        return field(f0, None, fi3, src, k, c, m, r)
-
-    fi3[...] = in3_ref[owner_ref[0] // RES].astype(F32)
-    take_block(owner_ref, blk, (IN3,), get)
+def shares_kernel(f0, face_ref, part, acc):
     acc[...] = part[...]
 
     def one_group(src, carry):
-        fi3[...] = in3_ref[src].astype(F32)
         for k in range(RES):
             scale = scale_of(f0, src, k)
             for z in (OUTER, INNER):
@@ -315,23 +309,42 @@
                     o = face_row(k, q, z)
                     got.append(face_ref[src, o:o + ROWS].astype(F32))
                 for n, r in enumerate(CORE_ROWS):
-                    v = [t[8 * n:8 * n + 8] for t in got]
-                    if z == INNER:
-                        far = [get(src, k, c, IN3, r) for c in range(COMPS)]
-                        for j in range(RES):
-                            re, im = densities(far, [blk[j, 0, c, r:r + 8] for c in range(COMPS)])
-                            v[2 * j] = v[2 * j] + re
-                            v[2 * j + 1] = v[2 * j + 1] + im
-                    a = [get(src, k, c, z, r) * scale for c in range(COMPS)]
-                    add_products(acc, z, r - H, a, v)
+                    a = [field(f0, None, None, src, k, c, z, r) * scale for c in range(COMPS)]
+                    add_products(acc, z, r - H, a, [t[8 * n:8 * n + 8] for t in got])
         return carry
 
     lax.fori_loop(0, GROUPS, one_group, 0)
+
+
+def join_kernel(core_ref, owner_ref, f0, in3_ref, part, out_ref, acc, fi3, blk):
+    def get(src, k, c, m, r):
+        return field(f0, None, fi3, src, k, c, m, r)
+
     core = core_ref[0]
+    fi3[...] = in3_ref[owner_ref[0] // RES].astype(F32)
+    take_block(owner_ref, blk, (IN3,), get)
     for j in range(RES):
         for c in range(COMPS):
-            out_ref[j, c, core] = acc[j, c, OUTER]
-            out_ref[j, c, 1 - core] = acc[j, c, INNER]
+            out_ref[j, c, core] = part[j, c, OUTER]
+            acc[j, c, 0] = part[j, c, INNER]
+
+    def one_group(src, carry):
+        fi3[...] = in3_ref[src].astype(F32)
+        for k in range(RES):
+            scale = scale_of(f0, src, k)
+            for r in CORE_ROWS:
+                far = [get(src, k, c, IN3, r) for c in range(COMPS)]
+                v = []
+                for j in range(RES):
+                    v.extend(densities(far, [blk[j, 0, c, r:r + 8] for c in range(COMPS)]))
+                a = [get(src, k, c, INNER, r) * scale for c in range(COMPS)]
+                add_products(acc, 0, r - H, a, v)
+        return carry
+
+    lax.fori_loop(0, GROUPS, one_group, 0)
+    for j in range(RES):
+        for c in range(COMPS):
+            out_ref[j, c, 1 - core] = acc[j, c, 0]
 
 
 INTERPRET = False
@@ -409,12 +422,15 @@
     )(block_owner, wide, in1, kept(den), kept(den1))
     in3 = shift(in3, -2, 2)
 
+    part = call(shares_kernel, made((RES, COMPS, PLANES, ROWS, LANES), F32), [vmem] * 3, [])(
+        wide, face, kept(part))
+
     return call(
         join_kernel, jax.ShapeDtypeStruct((RES, COMPS, PLANES, ROWS, LANES), F32),
-        [smem, smem] + [vmem] * 4,
-        [pltpu.VMEM((RES, COMPS, PLANES, ROWS, LANES), F32), pltpu.VMEM((N2, LANES), F32),
+        [smem, smem] + [vmem] * 3,
+        [pltpu.VMEM((RES, COMPS, 1, ROWS, LANES), F32), pltpu.VMEM((N2, LANES), F32),
          pltpu.VMEM((RES, 1, COMPS, 24, LANES), F32)],
-    )(core, block_owner, wide, in3, face, kept(part))
+    )(core, block_owner, wide, in3, kept(part))
 
 
 def solution(mesh):

time: 61.2 us -> 61 us (level)
  no operation moved by 1% of the time
where the time goes in v2:
time: 61 us; the launch traced here: 60.7 us
  blocking collectives  26.8 us (44%)
  starting transfers between devices  14.4 us (24%)
  Pallas kernels  11.1 us (18%)
  waiting for transfers between devices  7.75 us (13%)
  between operations  0.72 us (1%)
    all_to_all x1, blocking collectives, on_device(): own = kept(lax.all_to_all(send, 'band', 0, 0, tiled=True))  26.8 us
    ppermute x3, starting transfers between devices, shift(): value = lax.ppermute(value, 'space', pairs)  14.4 us
    ppermute x3, waiting for transfers between devices, shift(): value = lax.ppermute(value, 'space', pairs)  7.75 us
    pallas_call x1, Pallas kernels, on_device(): call(local_kernel, made((RES, COMPS, PLANES, ROWS, LANES), F32), [smem] +...  5.63 us
    pallas_call x1, Pallas kernels, on_device(): call(own_face_kernel, [made((GROUPS * RES, 2 * RES, 2, 24, LANES), F32),...  2 us
    pallas_call x1, Pallas kernels, on_device(): call(pack_kernel, made((GROUPS, SEND, LANES), BF16), [smem, hbm, hbm], [p...  1.31 us
  transfers between devices with their start and end apart: 3, of which 1 were waited for; matrix products, arithmetic and copies ran while one was open for 0% of the time, Pallas kernels for 13%

profile of v2, /device:TPU:1, one launch (start us, length us, event | category | flops | bytes accessed | tf_op | source)
XLA Modules:
  0.0 60.7 jit_solution(9109939034629208015)
XLA Ops:
  0.0 1.3 %shard_map.37 = bf16[8,360,128]{2,1,0:T(8,128)(2,1)S(1)} custom-call(s32[1]{0:T(128)} %bitcast.core_ref, bf16[16,128,128]{2,1,0:T(8,128)(2,1)} %bitcast.2, s32[2]{0:T(128)} %occ_hbm.1), custom_call_target="tpu_custom_call" | custom-call | tf_op jit(solution)/shard_map/pallas_call | solution.py:379
  1.3 26.8 %all_to_all.5.own_ref = bf16[8,360,128]{2,1,0:T(8,128)(2,1)S(1)} all-to-all(bf16[8,360,128]{2,1,0:T(8,128)(2,1)S(1)} %shard_map.37), channel_id=1, replica_groups=mesh['space'=64,'band'=8] {'band'}, dimensions={0} | all-to-all | bytes 1474560 | tf_op jit(solution)/shard_map/all_to_all | solution.py:385
  28.1 0.3 shard_map.38
  28.4 6.5 %collective-permute-start.1 = (bf16[8,304,128]{2,1,0:T(8,128)(2,1)S(1)}, bf16[8,304,128]{2,1,0:T(8,128)(2,1)S(1)}, u32[]{:S(2)}, u32[]{:S(2)}) collective-permute-start(bf16[8,304,128]{2,1,0:T(8,128)(2,1)S(1)} %get-tuple-element.15), channel_id=1, source_target_pairs={{0,8},{8,0},{16,24},{24,16},{32,40},{40,32},{48,56},{56,48},{64,72... | collective-permute-start | bytes 1867784 | tf_op jit(solution)/shard_map/ppermute | solution.py:397
  35.6 2.0 %shard_map.39 = (f32[16,4,2,24,128]{4,3,2,1,0:T(8,128)S(1)}, f32[8,256,128]{2,1,0:T(8,128)S(1)}) custom-call(s32[1]{0:T(128)S(6)} %copy.4.owner_ref, f32[8,360,128]{2,1,0:T(8,128)S(1)} %get-tuple-element.12.f0), custom_call_target="tpu_custom_call" | custom-call | tf_op jit(solution)/shard_map/pallas_call | solution.py:402
  37.6 0.0 collective-permute-done.1.in1_ref
  37.6 0.4 shard_map.40
  38.0 3.9 %collective-permute-start.2 = (bf16[8,256,128]{2,1,0:T(8,128)(2,1)S(1)}, bf16[8,256,128]{2,1,0:T(8,128)(2,1)S(1)}, u32[]{:S(2)}, u32[]{:S(2)}) collective-permute-start(bf16[8,256,128]{2,1,0:T(8,128)(2,1)S(1)} %get-tuple-element.16), channel_id=1, source_target_pairs={{0,504},{8,16},{16,8},{24,32},{32,24},{40,48},{48,40},{56,64},{64,... | collective-permute-start | bytes 1572872 | tf_op jit(solution)/shard_map/ppermute | solution.py:397
  41.9 4.0 %collective-permute-start = (bf16[8,128,128]{2,1,0:T(8,128)(2,1)S(1)}, bf16[8,128,128]{2,1,0:T(8,128)(2,1)S(1)}, u32[]{:S(2)}, u32[]{:S(2)}) collective-permute-start(bf16[8,128,128]{2,1,0:T(8,128)(2,1)S(1)} %get-tuple-element.13), channel_id=1, source_target_pairs={{0,496},{8,24},{16,0},{24,40},{32,16},{40,56},{48,32},{56,72},{64,... | collective-permute-start | bytes 786440 | tf_op jit(solution)/shard_map/ppermute | solution.py:397
  45.9 5.6 %shard_map.41.part = f32[2,4,2,16,128]{4,3,2,1,0:T(8,128)S(1)} custom-call(s32[1]{0:T(128)S(6)} %copy.4.owner_ref, f32[8,360,128]{2,1,0:T(8,128)S(1)} %get-tuple-element.12.f0, bf16[8,304,128]{2,1,0:T(8,128)(2,1)S(1)} %collective-permute-done.1.in1_ref, f32[16,4,2,24,128]{4,3,2,1,0:T(8,128)S(1)} %get-tuple-element.17.den, ...), custom_call_target="tpu_custom_call" | custom-call | tf_op jit(solution)/shard_map/pallas_call | solution.py:417
  51.5 0.0 collective-permute-done.2.face_ref
  51.6 0.4 shard_map.42.part
  52.0 7.7 %collective-permute-done.in3_ref = bf16[8,128,128]{2,1,0:T(8,128)(2,1)S(1)} collective-permute-done((bf16[8,128,128]{2,1,0:T(8,128)(2,1)S(1)}, bf16[8,128,128]{2,1,0:T(8,128)(2,1)S(1)}, u32[]{:S(2)}, u32[]{:S(2)}) %collective-permute-start) | collective-permute-done | bytes 262176 | tf_op jit(solution)/shard_map/ppermute | solution.py:397
  59.7 1.0 %shard_map.43 = f32[2,4,2,16,128]{4,3,2,1,0:T(8,128)} custom-call(s32[1]{0:T(128)} %bitcast.core_ref, s32[1]{0:T(128)S(6)} %copy.4.owner_ref, f32[8,360,128]{2,1,0:T(8,128)S(1)} %get-tuple-element.12.f0, bf16[8,128,128]{2,1,0:T(8,128)(2,1)S(1)} %collective-permute-done.in3_ref, f32[2,4,2,16,128]{4,3,2,1,0:T(8,128)S(1)} %shard_map.42.part), custom_call_target="tpu_custom_call" | custom-call | tf_op jit(solution)/shard_map/pallas_call | solution.py:428
Async XLA Ops:
  28.4 9.2 %collective-permute-start.1 = (bf16[8,304,128]{2,1,0:T(8,128)(2,1)S(1)}, bf16[8,304,128]{2,1,0:T(8,128)(2,1)S(1)}, u32[]{:S(2)}, u32[]{:S(2)}) collective-permute-start(bf16[8,304,128]{2,1,0:T(8,128)(2,1)S(1)} %get-tuple-element.15), channel_id=1, source_target_pairs={{0,8},{8,0},{16,24},{24,16},{32,40},{40,32},{48,56},{56,48},{64,72... | collective-permute-start | bytes 1867784 | tf_op jit(solution)/shard_map/ppermute | solution.py:397
  38.0 13.6 %collective-permute-start.2 = (bf16[8,256,128]{2,1,0:T(8,128)(2,1)S(1)}, bf16[8,256,128]{2,1,0:T(8,128)(2,1)S(1)}, u32[]{:S(2)}, u32[]{:S(2)}) collective-permute-start(bf16[8,256,128]{2,1,0:T(8,128)(2,1)S(1)} %get-tuple-element.16), channel_id=1, source_target_pairs={{0,504},{8,16},{16,8},{24,32},{32,24},{40,48},{48,40},{56,64},{64,... | collective-permute-start | bytes 1572872 | tf_op jit(solution)/shard_map/ppermute | solution.py:397
  41.9 17.8 %collective-permute-start = (bf16[8,128,128]{2,1,0:T(8,128)(2,1)S(1)}, bf16[8,128,128]{2,1,0:T(8,128)(2,1)S(1)}, u32[]{:S(2)}, u32[]{:S(2)}) collective-permute-start(bf16[8,128,128]{2,1,0:T(8,128)(2,1)S(1)} %get-tuple-element.13), channel_id=1, source_target_pairs={{0,496},{8,24},{16,0},{24,40},{32,16},{40,56},{48,32},{56,72},{64,... | collective-permute-start | bytes 786440 | tf_op jit(solution)/shard_map/ppermute | solution.py:397

commit v3 on v2

--- a/solution.py
+++ b/solution.py
@@ -154,7 +154,7 @@
     return pltpu.roll(t, 1, 1) + pltpu.roll(t, LANES - 1, 1)
 
 
-def own_face_kernel(owner_ref, f0, den, fab, blk, lap, us):
+def own_face_body(owner_ref, f0, den, fab, blk, lap, us):
     def get(src, k, c, m, r):
         return field(f0, None, None, src, k, c, m, r)
 
@@ -188,6 +188,14 @@
         return carry
 
     lax.fori_loop(0, GROUPS, one_group, 0)
+
+
+def own_odd_kernel(core_ref, *refs):
+    pl.when(core_ref[0] == 1)(lambda: own_face_body(*refs))
+
+
+def own_even_kernel(core_ref, owner_ref, f0, den_in, fab_in, *refs):
+    pl.when(core_ref[0] == 0)(lambda: own_face_body(owner_ref, f0, *refs))
 
 
 def face_kernel(owner_ref, fab, in1_ref, den1, face_ref, fi, blk):
@@ -366,11 +374,11 @@
     def in_hbm(value):
         return pltpu.with_memory_space_constraint(value, pltpu.HBM) if KEEP else value
 
-    def call(kernel, out_shape, in_specs, scratch):
+    def call(kernel, out_shape, in_specs, scratch, aliases={}):
         out_specs = [vmem] * len(out_shape) if isinstance(out_shape, list) else vmem
         return pl.pallas_call(
             kernel, out_shape=out_shape, in_specs=in_specs, out_specs=out_specs,
-            scratch_shapes=scratch, interpret=INTERPRET,
+            scratch_shapes=scratch, interpret=INTERPRET, input_output_aliases=aliases,
             compiler_params=pltpu.CompilerParams(vmem_limit_bytes=GRANT))
 
     x = bands.shape[3]
@@ -399,13 +407,13 @@
 
     in1 = shift(in1, 1, -1)
 
-    den, fab = call(
-        own_face_kernel,
-        [made((GROUPS * RES, 2 * RES, 2, 24, LANES), F32), made((GROUPS, NF, LANES), F32)],
-        [smem, vmem],
-        [pltpu.VMEM((RES, 2, COMPS, 24, LANES), F32), pltpu.VMEM((RES, 2 * RES, 24, LANES), F32),
-         pltpu.VMEM((RES, 2 * RES, 24, LANES), F32)],
-    )(block_owner, wide)
+    own_out = [made((GROUPS * RES, 2 * RES, 2, 24, LANES), F32), made((GROUPS, NF, LANES), F32)]
+    own_scratch = [pltpu.VMEM((RES, 2, COMPS, 24, LANES), F32), pltpu.VMEM((RES, 2 * RES, 24, LANES), F32),
+                   pltpu.VMEM((RES, 2 * RES, 24, LANES), F32)]
+    den, fab = call(own_odd_kernel, own_out, [smem, smem, vmem],
+                    own_scratch)(core, block_owner, wide)
+    den, fab = call(own_even_kernel, own_out, [smem, smem] + [vmem] * 3,
+                    own_scratch, {3: 0, 4: 1})(core, block_owner, wide, kept(den), kept(fab))
     den1, face = call(
         face_kernel,
         [made((GROUPS * RES, 2 * RES, 24, LANES), F32), made((GROUPS, NF, LANES), BF16)],

time: 61 us -> 61.1 us (level)
    pallas_call x1 -> x2, Pallas kernels: 2 us -> 2.02 us  [the longest x1 2.01 us: on_device(): call(own_odd_kernel, own_out, [smem, smem, vmem], own_scratch)]
where the time goes in v3:
time: 61.1 us; the launch traced here: 60.8 us
  blocking collectives  26.8 us (44%)
  starting transfers between devices  14.4 us (24%)
  Pallas kernels  11.2 us (18%)
  waiting for transfers between devices  7.71 us (13%)
  between operations  0.74 us (1%)
    all_to_all x1, blocking collectives, on_device(): own = kept(lax.all_to_all(send, 'band', 0, 0, tiled=True))  26.8 us
    ppermute x3, starting transfers between devices, shift(): value = lax.ppermute(value, 'space', pairs)  14.4 us
    ppermute x3, waiting for transfers between devices, shift(): value = lax.ppermute(value, 'space', pairs)  7.71 us
    pallas_call x1, Pallas kernels, on_device(): call(local_kernel, made((RES, COMPS, PLANES, ROWS, LANES), F32), [smem] +...  5.66 us
    pallas_call x1, Pallas kernels, on_device(): call(own_odd_kernel, own_out, [smem, smem, vmem], own_scratch)  2.01 us
    pallas_call x1, Pallas kernels, on_device(): call(pack_kernel, made((GROUPS, SEND, LANES), BF16), [smem, hbm, hbm], [p...  1.31 us
  transfers between devices with their start and end apart: 3, of which 1 were waited for; matrix products, arithmetic and copies ran while one was open for 0% of the time, Pallas kernels for 13%

profile of v3, /device:TPU:1, one launch (start us, length us, event | category | flops | bytes accessed | tf_op | source)
XLA Modules:
  0.0 60.8 jit_solution(17582698353922390156)
XLA Ops:
  0.0 1.3 %shard_map.37 = bf16[8,360,128]{2,1,0:T(8,128)(2,1)S(1)} custom-call(s32[1]{0:T(128)} %bitcast.core_ref, bf16[16,128,128]{2,1,0:T(8,128)(2,1)} %bitcast.2, s32[2]{0:T(128)} %occ_hbm.1), custom_call_target="tpu_custom_call" | custom-call | tf_op jit(solution)/shard_map/pallas_call | solution.py:387
  1.3 26.8 %all_to_all.5.own_ref = bf16[8,360,128]{2,1,0:T(8,128)(2,1)S(1)} all-to-all(bf16[8,360,128]{2,1,0:T(8,128)(2,1)S(1)} %shard_map.37), channel_id=1, replica_groups=mesh['space'=64,'band'=8] {'band'}, dimensions={0} | all-to-all | bytes 1474560 | tf_op jit(solution)/shard_map/all_to_all | solution.py:393
  28.1 0.3 shard_map.38
  28.4 6.5 %collective-permute-start.1 = (bf16[8,304,128]{2,1,0:T(8,128)(2,1)S(1)}, bf16[8,304,128]{2,1,0:T(8,128)(2,1)S(1)}, u32[]{:S(2)}, u32[]{:S(2)}) collective-permute-start(bf16[8,304,128]{2,1,0:T(8,128)(2,1)S(1)} %get-tuple-element.19), channel_id=1, source_target_pairs={{0,8},{8,0},{16,24},{24,16},{32,40},{40,32},{48,56},{56,48},{64,72... | collective-permute-start | bytes 1867784 | tf_op jit(solution)/shard_map/ppermute | solution.py:405
  35.6 2.0 %shard_map.39 = (f32[16,4,2,24,128]{4,3,2,1,0:T(8,128)S(1)}, f32[8,256,128]{2,1,0:T(8,128)S(1)}) custom-call(s32[1]{0:T(128)} %bitcast.core_ref, s32[1]{0:T(128)S(6)} %copy.8.refs_0_.owner_ref, f32[8,360,128]{2,1,0:T(8,128)S(1)} %get-tuple-element.14.refs_1_.f0), custom_call_target="tpu_custom_call" | custom-call | tf_op jit(solution)/shard_map/pallas_call | solution.py:413
  37.6 0.0 collective-permute-done.1.in1_ref
  37.6 0.4 shard_map.41
  38.0 3.9 %collective-permute-start.2 = (bf16[8,256,128]{2,1,0:T(8,128)(2,1)S(1)}, bf16[8,256,128]{2,1,0:T(8,128)(2,1)S(1)}, u32[]{:S(2)}, u32[]{:S(2)}) collective-permute-start(bf16[8,256,128]{2,1,0:T(8,128)(2,1)S(1)} %get-tuple-element.20), channel_id=1, source_target_pairs={{0,504},{8,16},{16,8},{24,32},{32,24},{40,48},{48,40},{56,64},{64,... | collective-permute-start | bytes 1572872 | tf_op jit(solution)/shard_map/ppermute | solution.py:405
  41.9 4.0 %collective-permute-start = (bf16[8,128,128]{2,1,0:T(8,128)(2,1)S(1)}, bf16[8,128,128]{2,1,0:T(8,128)(2,1)S(1)}, u32[]{:S(2)}, u32[]{:S(2)}) collective-permute-start(bf16[8,128,128]{2,1,0:T(8,128)(2,1)S(1)} %get-tuple-element.15), channel_id=1, source_target_pairs={{0,496},{8,24},{16,0},{24,40},{32,16},{40,56},{48,32},{56,72},{64,... | collective-permute-start | bytes 786440 | tf_op jit(solution)/shard_map/ppermute | solution.py:405
  46.0 5.7 %shard_map.42.part = f32[2,4,2,16,128]{4,3,2,1,0:T(8,128)S(1)} custom-call(s32[1]{0:T(128)S(6)} %copy.8.refs_0_.owner_ref, f32[8,360,128]{2,1,0:T(8,128)S(1)} %get-tuple-element.14.refs_1_.f0, bf16[8,304,128]{2,1,0:T(8,128)(2,1)S(1)} %collective-permute-done.1.in1_ref, f32[16,4,2,24,128]{4,3,2,1,0:T(8,128)S(1)} %get-tuple-element.21.den, ...), custom_call_target="tpu_custom_call" | custom-call | tf_op jit(solution)/shard_map/pallas_call | solution.py:425
  51.6 0.0 collective-permute-done.2.face_ref
  51.6 0.4 shard_map.43.part
  52.1 7.7 %collective-permute-done.in3_ref = bf16[8,128,128]{2,1,0:T(8,128)(2,1)S(1)} collective-permute-done((bf16[8,128,128]{2,1,0:T(8,128)(2,1)S(1)}, bf16[8,128,128]{2,1,0:T(8,128)(2,1)S(1)}, u32[]{:S(2)}, u32[]{:S(2)}) %collective-permute-start) | collective-permute-done | bytes 262176 | tf_op jit(solution)/shard_map/ppermute | solution.py:405
  59.8 1.0 %shard_map.44 = f32[2,4,2,16,128]{4,3,2,1,0:T(8,128)} custom-call(s32[1]{0:T(128)} %bitcast.core_ref, s32[1]{0:T(128)S(6)} %copy.8.refs_0_.owner_ref, f32[8,360,128]{2,1,0:T(8,128)S(1)} %get-tuple-element.14.refs_1_.f0, bf16[8,128,128]{2,1,0:T(8,128)(2,1)S(1)} %collective-permute-done.in3_ref, f32[2,4,2,16,128]{4,3,2,1,0:T(8,128)S(1)} %shard_map.43.part), custom_call_target="tpu_custom_call" | custom-call | tf_op jit(solution)/shard_map/pallas_call | solution.py:436
  (1 shorter events, 0.0 us)
Async XLA Ops:
  28.4 9.2 %collective-permute-start.1 = (bf16[8,304,128]{2,1,0:T(8,128)(2,1)S(1)}, bf16[8,304,128]{2,1,0:T(8,128)(2,1)S(1)}, u32[]{:S(2)}, u32[]{:S(2)}) collective-permute-start(bf16[8,304,128]{2,1,0:T(8,128)(2,1)S(1)} %get-tuple-element.19), channel_id=1, source_target_pairs={{0,8},{8,0},{16,24},{24,16},{32,40},{40,32},{48,56},{56,48},{64,72... | collective-permute-start | bytes 1867784 | tf_op jit(solution)/shard_map/ppermute | solution.py:405
  38.0 13.6 %collective-permute-start.2 = (bf16[8,256,128]{2,1,0:T(8,128)(2,1)S(1)}, bf16[8,256,128]{2,1,0:T(8,128)(2,1)S(1)}, u32[]{:S(2)}, u32[]{:S(2)}) collective-permute-start(bf16[8,256,128]{2,1,0:T(8,128)(2,1)S(1)} %get-tuple-element.20), channel_id=1, source_target_pairs={{0,504},{8,16},{16,8},{24,32},{32,24},{40,48},{48,40},{56,64},{64,... | collective-permute-start | bytes 1572872 | tf_op jit(solution)/shard_map/ppermute | solution.py:405
  41.9 17.8 %collective-permute-start = (bf16[8,128,128]{2,1,0:T(8,128)(2,1)S(1)}, bf16[8,128,128]{2,1,0:T(8,128)(2,1)S(1)}, u32[]{:S(2)}, u32[]{:S(2)}) collective-permute-start(bf16[8,128,128]{2,1,0:T(8,128)(2,1)S(1)} %get-tuple-element.15), channel_id=1, source_target_pairs={{0,496},{8,24},{16,0},{24,40},{32,16},{40,56},{48,32},{56,72},{64,... | collective-permute-start | bytes 786440 | tf_op jit(solution)/shard_map/ppermute | solution.py:405

commit v4 on v2

--- a/solution.py
+++ b/solution.py
@@ -75,12 +75,12 @@
             ext[n, 0:8] = t[x - 8:x]
             ext[n, 8 + x:16 + x] = t[0:8]
     levels.wait()
-    for k in range(RES):
-        flat[BODY + 4 * k:BODY + 4 * k + 4] = jnp.full((4, LANES), occ_ref[k].astype(F32), F32)
     for b in range(GROUPS):
+        for k in range(RES):
+            flat[b, BODY + 4 * k:BODY + 4 * k + 4] = jnp.full((4, LANES), occ_ref[k].astype(F32), F32)
         for n in range(PLANES * RES * COMPS):
-            flat[n * WIN:(n + 1) * WIN] = ext[n, ROWS * b + 8 - H:ROWS * b + 8 - H + WIN]
-        out_ref[b] = flat[...].astype(BF16)
+            flat[b, n * WIN:(n + 1) * WIN] = ext[n, ROWS * b + 8 - H:ROWS * b + 8 - H + WIN]
+        out_ref[b] = flat[b].astype(BF16)
 
 
 def cut_kernel(own_ref, wide_ref, in1_ref, in3_ref, s1, s4):
@@ -236,7 +236,8 @@
         return field(f0, fi, None, src, k, c, m, r)
 
     def widen(src):
-        fi[...] = in1_ref[src].astype(F32)
+        near = mid_row(0, 0)
+        fi[near:N1] = in1_ref[src, near:N1].astype(F32)
 
     planes = (IN2,)
     widen(owner_ref[0] // RES)
@@ -379,7 +380,7 @@
     send = call(
         pack_kernel, made((GROUPS, SEND, LANES), BF16), [smem, hbm, hbm],
         [pltpu.VMEM((RES * COMPS * PLANES, x, LANES), BF16), pltpu.SMEM((RES,), jnp.int32),
-         pltpu.VMEM((PLANES * RES * COMPS, x + 16, LANES), F32), pltpu.VMEM((SEND, LANES), F32),
+         pltpu.VMEM((PLANES * RES * COMPS, x + 16, LANES), F32), pltpu.VMEM((GROUPS, SEND, LANES), F32),
          pltpu.SemaphoreType.DMA((RES * COMPS,)), pltpu.SemaphoreType.DMA],
     )(core, in_hbm(bands.reshape(RES * COMPS * PLANES, x, LANES)), in_hbm(occ_level))
     own = kept(lax.all_to_all(send, "band", 0, 0, tiled=True))

time: 61 us -> 61 us (level)
  no operation moved by 1% of the time
where the time goes in v4:
time: 61 us; the launch traced here: 60.7 us
  blocking collectives  26.8 us (44%)
  starting transfers between devices  14.4 us (24%)
  Pallas kernels  11.1 us (18%)
  waiting for transfers between devices  7.75 us (13%)
  between operations  0.72 us (1%)
    all_to_all x1, blocking collectives, on_device(): own = kept(lax.all_to_all(send, 'band', 0, 0, tiled=True))  26.8 us
    ppermute x3, starting transfers between devices, shift(): value = lax.ppermute(value, 'space', pairs)  14.4 us
    ppermute x3, waiting for transfers between devices, shift(): value = lax.ppermute(value, 'space', pairs)  7.75 us
    pallas_call x1, Pallas kernels, on_device(): call(local_kernel, made((RES, COMPS, PLANES, ROWS, LANES), F32), [smem] +...  5.63 us
    pallas_call x1, Pallas kernels, on_device(): call(own_face_kernel, [made((GROUPS * RES, 2 * RES, 2, 24, LANES), F32),...  2 us
    pallas_call x1, Pallas kernels, on_device(): call(pack_kernel, made((GROUPS, SEND, LANES), BF16), [smem, hbm, hbm], [p...  1.32 us
  transfers between devices with their start and end apart: 3, of which 1 were waited for; matrix products, arithmetic and copies ran while one was open for 0% of the time, Pallas kernels for 13%

profile of v4, /device:TPU:1, one launch (start us, length us, event | category | flops | bytes accessed | tf_op | source)
XLA Modules:
  0.0 60.7 jit_solution(6595695500586827919)
XLA Ops:
  0.0 1.3 %shard_map.37 = bf16[8,360,128]{2,1,0:T(8,128)(2,1)S(1)} custom-call(s32[1]{0:T(128)} %bitcast.core_ref, bf16[16,128,128]{2,1,0:T(8,128)(2,1)} %bitcast.2, s32[2]{0:T(128)} %occ_hbm.1), custom_call_target="tpu_custom_call" | custom-call | tf_op jit(solution)/shard_map/pallas_call | solution.py:380
  1.3 26.8 %all_to_all.5.own_ref = bf16[8,360,128]{2,1,0:T(8,128)(2,1)S(1)} all-to-all(bf16[8,360,128]{2,1,0:T(8,128)(2,1)S(1)} %shard_map.37), channel_id=1, replica_groups=mesh['space'=64,'band'=8] {'band'}, dimensions={0} | all-to-all | bytes 1474560 | tf_op jit(solution)/shard_map/all_to_all | solution.py:386
  28.1 0.3 shard_map.38
  28.4 6.5 %collective-permute-start.1 = (bf16[8,304,128]{2,1,0:T(8,128)(2,1)S(1)}, bf16[8,304,128]{2,1,0:T(8,128)(2,1)S(1)}, u32[]{:S(2)}, u32[]{:S(2)}) collective-permute-start(bf16[8,304,128]{2,1,0:T(8,128)(2,1)S(1)} %get-tuple-element.15), channel_id=1, source_target_pairs={{0,8},{8,0},{16,24},{24,16},{32,40},{40,32},{48,56},{56,48},{64,72... | collective-permute-start | bytes 1867784 | tf_op jit(solution)/shard_map/ppermute | solution.py:398
  35.6 2.0 %shard_map.39 = (f32[16,4,2,24,128]{4,3,2,1,0:T(8,128)S(1)}, f32[8,256,128]{2,1,0:T(8,128)S(1)}) custom-call(s32[1]{0:T(128)S(6)} %copy.4.owner_ref, f32[8,360,128]{2,1,0:T(8,128)S(1)} %get-tuple-element.12.f0), custom_call_target="tpu_custom_call" | custom-call | tf_op jit(solution)/shard_map/pallas_call | solution.py:403
  37.6 0.0 collective-permute-done.1.in1_ref
  37.6 0.4 shard_map.40
  38.0 3.9 %collective-permute-start.2 = (bf16[8,256,128]{2,1,0:T(8,128)(2,1)S(1)}, bf16[8,256,128]{2,1,0:T(8,128)(2,1)S(1)}, u32[]{:S(2)}, u32[]{:S(2)}) collective-permute-start(bf16[8,256,128]{2,1,0:T(8,128)(2,1)S(1)} %get-tuple-element.16), channel_id=1, source_target_pairs={{0,504},{8,16},{16,8},{24,32},{32,24},{40,48},{48,40},{56,64},{64,... | collective-permute-start | bytes 1572872 | tf_op jit(solution)/shard_map/ppermute | solution.py:398
  41.9 4.0 %collective-permute-start = (bf16[8,128,128]{2,1,0:T(8,128)(2,1)S(1)}, bf16[8,128,128]{2,1,0:T(8,128)(2,1)S(1)}, u32[]{:S(2)}, u32[]{:S(2)}) collective-permute-start(bf16[8,128,128]{2,1,0:T(8,128)(2,1)S(1)} %get-tuple-element.13), channel_id=1, source_target_pairs={{0,496},{8,24},{16,0},{24,40},{32,16},{40,56},{48,32},{56,72},{64,... | collective-permute-start | bytes 786440 | tf_op jit(solution)/shard_map/ppermute | solution.py:398
  45.9 5.6 %shard_map.41.part = f32[2,4,2,16,128]{4,3,2,1,0:T(8,128)S(1)} custom-call(s32[1]{0:T(128)S(6)} %copy.4.owner_ref, f32[8,360,128]{2,1,0:T(8,128)S(1)} %get-tuple-element.12.f0, bf16[8,304,128]{2,1,0:T(8,128)(2,1)S(1)} %collective-permute-done.1.in1_ref, f32[16,4,2,24,128]{4,3,2,1,0:T(8,128)S(1)} %get-tuple-element.17.den, ...), custom_call_target="tpu_custom_call" | custom-call | tf_op jit(solution)/shard_map/pallas_call | solution.py:418
  51.6 0.0 collective-permute-done.2.face_ref
  51.6 0.4 shard_map.42.part
  52.0 7.7 %collective-permute-done.in3_ref = bf16[8,128,128]{2,1,0:T(8,128)(2,1)S(1)} collective-permute-done((bf16[8,128,128]{2,1,0:T(8,128)(2,1)S(1)}, bf16[8,128,128]{2,1,0:T(8,128)(2,1)S(1)}, u32[]{:S(2)}, u32[]{:S(2)}) %collective-permute-start) | collective-permute-done | bytes 262176 | tf_op jit(solution)/shard_map/ppermute | solution.py:398
  59.7 1.0 %shard_map.43 = f32[2,4,2,16,128]{4,3,2,1,0:T(8,128)} custom-call(s32[1]{0:T(128)} %bitcast.core_ref, s32[1]{0:T(128)S(6)} %copy.4.owner_ref, f32[8,360,128]{2,1,0:T(8,128)S(1)} %get-tuple-element.12.f0, bf16[8,128,128]{2,1,0:T(8,128)(2,1)S(1)} %collective-permute-done.in3_ref, f32[2,4,2,16,128]{4,3,2,1,0:T(8,128)S(1)} %shard_map.42.part), custom_call_target="tpu_custom_call" | custom-call | tf_op jit(solution)/shard_map/pallas_call | solution.py:429
Async XLA Ops:
  28.4 9.2 %collective-permute-start.1 = (bf16[8,304,128]{2,1,0:T(8,128)(2,1)S(1)}, bf16[8,304,128]{2,1,0:T(8,128)(2,1)S(1)}, u32[]{:S(2)}, u32[]{:S(2)}) collective-permute-start(bf16[8,304,128]{2,1,0:T(8,128)(2,1)S(1)} %get-tuple-element.15), channel_id=1, source_target_pairs={{0,8},{8,0},{16,24},{24,16},{32,40},{40,32},{48,56},{56,48},{64,72... | collective-permute-start | bytes 1867784 | tf_op jit(solution)/shard_map/ppermute | solution.py:398
  38.0 13.6 %collective-permute-start.2 = (bf16[8,256,128]{2,1,0:T(8,128)(2,1)S(1)}, bf16[8,256,128]{2,1,0:T(8,128)(2,1)S(1)}, u32[]{:S(2)}, u32[]{:S(2)}) collective-permute-start(bf16[8,256,128]{2,1,0:T(8,128)(2,1)S(1)} %get-tuple-element.16), channel_id=1, source_target_pairs={{0,504},{8,16},{16,8},{24,32},{32,24},{40,48},{48,40},{56,64},{64,... | collective-permute-start | bytes 1572872 | tf_op jit(solution)/shard_map/ppermute | solution.py:398
  41.9 17.8 %collective-permute-start = (bf16[8,128,128]{2,1,0:T(8,128)(2,1)S(1)}, bf16[8,128,128]{2,1,0:T(8,128)(2,1)S(1)}, u32[]{:S(2)}, u32[]{:S(2)}) collective-permute-start(bf16[8,128,128]{2,1,0:T(8,128)(2,1)S(1)} %get-tuple-element.13), channel_id=1, source_target_pairs={{0,496},{8,24},{16,0},{24,40},{32,16},{40,56},{48,32},{56,72},{64,... | collective-permute-start | bytes 786440 | tf_op jit(solution)/shard_map/ppermute | solution.py:398
